TPU v7x, 128 devices: a whole 4x4x4 slice. The times are simulated.
128 devices in a mesh: grp: 8 (over y, core), dev: 16 (over x, z).
Axes of the slice: x: 4, y: 4, z: 4, core: 2. Of those that a mesh axis runs over, the one named last changes fastest.
Arguments:
- tiles: bfloat16 [65536, 128, 128], P(('grp', 'dev')), may hold values from -0.125 to 0.125
- tile_ray: int32 [65536], P(('grp', 'dev')), may hold values from 0 to 31, as said below
- tile_col: int32 [65536], P(('grp', 'dev')), may hold values from 0 to 23, as said below
- touched: int32 [3072], P(('grp', 'dev')), may hold values from 0 to 8191, as said below
- home: int32 [8192], replicated, may hold values from 0 to 8191, as said below
- sketch: bfloat16 [1048576, 128], P(('grp', 'dev')), may hold values from -6 to 6
Outputs:
- basis: float32 [1048576, 128], P(('grp', 'dev'))
- r_factor: float32 [128, 128], replicated
Inputs may be any that keep to these rules, and one draw needn't show every extreme that they name: `home`: A permutation that maps each region of 1024 consecutive voxel blocks, g * 1024 to (g + 1) * 1024 - 1, onto the same range of positions. The 24 entries of device i along grp+dev are distinct voxel blocks whose positions home[v] lie in the region of its group g = i // 16; at most 3 of them have positions stored on any one device (position // 64), and in every group one device stores 3 of the touched blocks of every device of the group. On each device the pairs (tile_ray, tile_col) are distinct. `tile_col`: indexes the device's own 24 entries of touched.
All inputs are finite; a program needn't handle non-finite values.
Results may differ from a plain program's by a relative error of at most 0.0017.
Values may be sent and summed in bfloat16 or wider, within the bound.
A program may use at most 192 MiB of HBM per device.

v0:
```python
import jax
import jax.numpy as jnp
from jax import lax
from jax.sharding import PartitionSpec as P

CAP = 3
RB_DEV = 32
gram_shift = 0.001


def factor_lower(gram_matrix):
    width = gram_matrix.shape[0]
    indices = jnp.arange(width, dtype=jnp.int32)

    def column_step(column, lower):
        pick = (indices == column).astype(jnp.float32)
        row_part = jnp.dot(pick, lower, precision=lax.Precision.HIGHEST)
        target = jnp.dot(gram_matrix, pick, precision=lax.Precision.HIGHEST)
        rest = target - jnp.dot(lower, row_part, precision=lax.Precision.HIGHEST)
        diagonal = jnp.sqrt(jnp.sum(rest * pick))
        fresh = jnp.where(
            indices > column, rest / diagonal, jnp.where(indices == column, diagonal, 0.0)
        )
        return lower + fresh[:, None] * pick[None, :]

    return lax.fori_loop(0, width, column_step, jnp.zeros((width, width), jnp.float32))


def invert_lower(lower):
    width = lower.shape[0]
    indices = jnp.arange(width, dtype=jnp.int32)

    def row_step(row, inverse):
        pick = (indices == row).astype(jnp.float32)
        row_part = jnp.dot(pick, lower, precision=lax.Precision.HIGHEST)
        diagonal = jnp.sum(row_part * pick)
        fresh = (pick - jnp.dot(row_part, inverse, precision=lax.Precision.HIGHEST)) / diagonal
        return inverse + pick[:, None] * fresh[None, :]

    return lax.fori_loop(0, width, row_step, jnp.zeros((width, width), jnp.float32))


def local(tiles, tile_ray, tile_col, touched, home, sketch):
    group_size = lax.axis_size("dev")
    tile_size = tiles.shape[1]
    width = sketch.shape[1]
    block_count = sketch.shape[0] // tile_size
    ntouch = touched.shape[0]
    slot_count = group_size * CAP
    matches = touched[:, None] == jnp.arange(home.shape[0], dtype=jnp.int32)[None, :]
    stored = jnp.sum(jnp.where(matches, home[None, :], 0), axis=1)
    holder = stored // block_count % group_size
    local_row = stored % block_count
    counter = jnp.arange(ntouch, dtype=jnp.int32)
    earlier = (holder[:, None] == holder[None, :]) & (counter[:, None] > counter[None, :])
    position = holder * CAP + jnp.sum(earlier, axis=1)
    placing = position[:, None] == jnp.arange(slot_count, dtype=jnp.int32)[None, :]
    request = (jnp.sum(jnp.where(placing, local_row[:, None] + 1, 0), axis=0) - 1).reshape(
        group_size, CAP
    )
    incoming = lax.all_to_all(request, "dev", split_axis=0, concat_axis=0, tiled=True)
    region_block = stored % (group_size * block_count)
    wanted = region_block[:, None] * tile_size + jnp.arange(tile_size, dtype=jnp.int32)[None, :]
    blank_rows = jnp.zeros((ntouch, tile_size, width), sketch.dtype)
    shard_rows = lax.all_gather(sketch, "dev", axis=0, tiled=True)
    length = shard_rows.shape[0]
    inside = (wanted >= 0) & (wanted < length)
    picked = jnp.take(shard_rows, jnp.clip(wanted, 0, length - 1).reshape(-1), axis=0).reshape(
        ntouch, tile_size, width
    )
    touched_rows = jnp.where(inside[:, :, None], picked, blank_rows)
    batch_rows = min(128, tiles.shape[0])
    rounds = tiles.shape[0] // batch_rows
    tile_steps = tiles.reshape(rounds, batch_rows, tile_size, tile_size)
    ray_steps = tile_ray.reshape(rounds, batch_rows)
    col_steps = tile_col.reshape(rounds, batch_rows)

    def image_step(running, inputs):
        tile_block, ray_block, col_block = inputs
        gathered = jnp.take(touched_rows, col_block, axis=0)
        product = jnp.einsum(
            "tab,tbk->tak", tile_block, gathered, preferred_element_type=jnp.float32
        )
        return (running.at[ray_block].add(product), None)

    images, _ = lax.scan(
        image_step,
        jnp.zeros((RB_DEV, tile_size, width), jnp.float32),
        (tile_steps, ray_steps, col_steps),
    )
    images = images.astype(jnp.bfloat16)

    def normal_step(running, inputs):
        tile_block, ray_block, col_block = inputs
        gathered = jnp.take(images, ray_block, axis=0)
        product = jnp.einsum(
            "tab,tak->tbk", tile_block, gathered, preferred_element_type=jnp.float32
        )
        return (running.at[col_block].add(product), None)

    partial_value, _ = lax.scan(
        normal_step,
        jnp.zeros((ntouch, tile_size, width), jnp.float32),
        (tile_steps, ray_steps, col_steps),
    )
    slot_of = jnp.sum(
        jnp.where(placing, jnp.arange(slot_count, dtype=jnp.int32)[None, :], 0), axis=1
    )
    outgoing = jnp.zeros((slot_count, tile_size, width), jnp.float32).at[slot_of].set(partial_value)
    arrived = lax.all_to_all(
        outgoing.reshape(group_size, CAP, tile_size, width),
        "dev",
        split_axis=0,
        concat_axis=0,
        tiled=True,
    )
    target = incoming.reshape(-1)
    safe_target = jnp.where(target >= 0, target, block_count)
    normal = (
        jnp.zeros((block_count + 1, tile_size, width), jnp.float32)
        .at[safe_target]
        .add(arrived.reshape(slot_count, tile_size, width))
    )
    normal = normal[:block_count].reshape(block_count * tile_size, width)
    gram_matrix = lax.psum(
        jnp.dot(normal.T, normal, precision=lax.Precision.HIGHEST), ("grp", "dev")
    )
    voxels = normal.shape[0] * lax.axis_size("grp") * group_size
    gram_matrix = gram_matrix / voxels + gram_shift * jnp.eye(width, dtype=jnp.float32)
    lower = factor_lower(gram_matrix)
    r_factor = lower.T
    inverse = invert_lower(lower).T
    basis_out = jnp.dot(normal, inverse, precision=lax.Precision.HIGHEST)
    return (basis_out, r_factor)


def solution(mesh):
    in_specs = (
        P(("grp", "dev"), None, None),
        P(("grp", "dev")),
        P(("grp", "dev")),
        P(("grp", "dev")),
        P(),
        P(("grp", "dev"), None),
    )
    out_specs = (P(("grp", "dev"), None), P())
    return jax.shard_map(local, mesh=mesh, in_specs=in_specs, out_specs=out_specs, check_vma=False)
```

profile of v0, /device:TPU:1, one launch (start us, length us, event | category | flops | bytes accessed | tf_op | source)
XLA Modules:
  0.0 1193.9 jit_solution(2345552403613061761)
XLA Ops:
  7.9 1.0 select_reduce_fusion
  10.0 8.5 all-to-all-start
  18.5 21.4 %copy.22 = bf16[512,128,128]{1,2,0:T(8,128)(2,1)} copy(bf16[512,128,128]{2,1,0:T(8,128)(2,1)} %param.14) | data formatting | bytes 33554432 | tf_op args[0]
  40.1 170.2 %all-gather.2.cloned.1.call-done = bf16[131072,128]{1,0:T(8,128)(2,1)} async-done(((bf16[8192,128]{1,0:T(8,128)(2,1)}), bf16[131072,128]{1,0:T(8,128)(2,1)}) %all-gather.2.cloned.1.call-update) | async-done | bytes 33554448 | tf_op jit(solution)/shard_map/all_gather | solution.py:65
  210.3 32.8 %gather_fusion.2 = bf16[3072,128]{1,0:T(8,128)(2,1)S(1)} fusion(bf16[131072,128]{1,0:T(8,128)(2,1)} %all-gather.2.cloned.1.call-done, s32[3072]{0:T(1024)S(1)} %broadcast_clamp_fusion), kind=kCustom, calls=%fused_computation.2 | custom fusion | bytes 1585152 | tf_op jit(solution)/shard_map/jit(_take)/gather | solution.py:68
  243.1 1.2 select_select_fusion
  244.6 113.0 %while.49 = (s32[]{:T(128)}, f32[32,128,128]{2,1,0:T(8,128)S(1)}, s32[4,128]{1,0:T(4,128)S(1)}, bf16[4,128,128,128]{3,2,1,0:T(8,128)(2,1)}, s32[4,128]{1,0:T(4,1...) while((s32[]{:T(128)}, f32[32,128,128]{2,1,0:T(8,128)S(1)}, s32[4,128]{1,0:T(4,128)S(1)}, ...), condition=%wide.region_6.7_spmd, body=%wide.region_4.6_spmd.sunk | while | flops 541067776 | bytes 50340692 | solution.py:86
  244.6 3.1 gather_fusion
  247.7 8.0 fusion.97
  255.7 17.1 %scatter_fusion = f32[32,128,128]{2,1,0:T(8,128)S(1)} fusion(f32[32,128,128]{2,1,0:T(8,128)S(1)} %get-tuple-element.482, s32[128]{0:T(128)S(1)} %get-tuple-element.454, f32[128,128,128]{2,1,0:T(8,128)} %fusion.97), kind=kCustom, calls=%fused_computation.3.clone.1 | custom fusion | flops 2097152 | bytes 25166336 | tf_op jit(solution)/shard_map/while/body/eval_jaxpr/scatter-add | solution.py:84
  272.8 3.1 gather_fusion
  276.0 8.0 fusion.97
  284.0 17.1 %scatter_fusion = f32[32,128,128]{2,1,0:T(8,128)S(1)} fusion(f32[32,128,128]{2,1,0:T(8,128)S(1)} %get-tuple-element.482, s32[128]{0:T(128)S(1)} %get-tuple-element.454, f32[128,128,128]{2,1,0:T(8,128)} %fusion.97), kind=kCustom, calls=%fused_computation.3.clone.1 | custom fusion | flops 2097152 | bytes 25166336 | tf_op jit(solution)/shard_map/while/body/eval_jaxpr/scatter-add | solution.py:84
  301.1 3.1 gather_fusion
  304.2 8.0 fusion.97
  312.2 17.1 %scatter_fusion = f32[32,128,128]{2,1,0:T(8,128)S(1)} fusion(f32[32,128,128]{2,1,0:T(8,128)S(1)} %get-tuple-element.482, s32[128]{0:T(128)S(1)} %get-tuple-element.454, f32[128,128,128]{2,1,0:T(8,128)} %fusion.97), kind=kCustom, calls=%fused_computation.3.clone.1 | custom fusion | flops 2097152 | bytes 25166336 | tf_op jit(solution)/shard_map/while/body/eval_jaxpr/scatter-add | solution.py:84
  329.3 3.1 gather_fusion
  332.4 8.0 fusion.97
  340.5 17.0 %scatter_fusion = f32[32,128,128]{2,1,0:T(8,128)S(1)} fusion(f32[32,128,128]{2,1,0:T(8,128)S(1)} %get-tuple-element.482, s32[128]{0:T(128)S(1)} %get-tuple-element.454, f32[128,128,128]{2,1,0:T(8,128)} %fusion.97), kind=kCustom, calls=%fused_computation.3.clone.1 | custom fusion | flops 2097152 | bytes 25166336 | tf_op jit(solution)/shard_map/while/body/eval_jaxpr/scatter-add | solution.py:84
  357.9 112.9 %while.50 = (s32[]{:T(128)}, f32[24,128,128]{2,1,0:T(8,128)S(1)}, s32[4,128]{1,0:T(4,128)S(1)}, bf16[4,128,128,128]{2,3,1,0:T(8,128)(2,1)}, s32[4,128]{1,0:T(4,1...) while((s32[]{:T(128)}, f32[24,128,128]{2,1,0:T(8,128)S(1)}, s32[4,128]{1,0:T(4,128)S(1)}, ...), condition=%wide.region_9.10_spmd, body=%wide.region_7.9_spmd.sunk | while | flops 541067776 | bytes 50340692 | solution.py:101
  357.9 3.1 gather_fusion.1
  361.0 8.0 fusion.101
  369.0 17.0 %scatter_fusion.1 = f32[24,128,128]{2,1,0:T(8,128)S(1)} fusion(f32[24,128,128]{2,1,0:T(8,128)S(1)} %get-tuple-element.503, s32[128]{0:T(128)S(1)} %get-tuple-element.462, f32[128,128,128]{2,1,0:T(8,128)} %fusion.101), kind=kCustom, calls=%fused_computation.4.clone.1 | custom fusion | flops 2097152 | bytes 25166336 | tf_op jit(solution)/shard_map/while/body/eval_jaxpr/scatter-add | solution.py:99
  386.1 3.1 gather_fusion.1
  389.2 8.0 fusion.101
  397.3 17.1 %scatter_fusion.1 = f32[24,128,128]{2,1,0:T(8,128)S(1)} fusion(f32[24,128,128]{2,1,0:T(8,128)S(1)} %get-tuple-element.503, s32[128]{0:T(128)S(1)} %get-tuple-element.462, f32[128,128,128]{2,1,0:T(8,128)} %fusion.101), kind=kCustom, calls=%fused_computation.4.clone.1 | custom fusion | flops 2097152 | bytes 25166336 | tf_op jit(solution)/shard_map/while/body/eval_jaxpr/scatter-add | solution.py:99
  414.4 3.1 gather_fusion.1
  417.5 8.0 fusion.101
  425.5 17.0 %scatter_fusion.1 = f32[24,128,128]{2,1,0:T(8,128)S(1)} fusion(f32[24,128,128]{2,1,0:T(8,128)S(1)} %get-tuple-element.503, s32[128]{0:T(128)S(1)} %get-tuple-element.462, f32[128,128,128]{2,1,0:T(8,128)} %fusion.101), kind=kCustom, calls=%fused_computation.4.clone.1 | custom fusion | flops 2097152 | bytes 25166336 | tf_op jit(solution)/shard_map/while/body/eval_jaxpr/scatter-add | solution.py:99
  442.6 3.1 gather_fusion.1
  445.7 8.0 fusion.101
  453.7 17.0 %scatter_fusion.1 = f32[24,128,128]{2,1,0:T(8,128)S(1)} fusion(f32[24,128,128]{2,1,0:T(8,128)S(1)} %get-tuple-element.503, s32[128]{0:T(128)S(1)} %get-tuple-element.462, f32[128,128,128]{2,1,0:T(8,128)} %fusion.101), kind=kCustom, calls=%fused_computation.4.clone.1 | custom fusion | flops 2097152 | bytes 25166336 | tf_op jit(solution)/shard_map/while/body/eval_jaxpr/scatter-add | solution.py:99
  470.8 2.0 broadcast_in_dim.133
  472.8 5.4 scatter_fusion.2
  478.3 4.9 all-to-all-start.1
  484.0 1.4 reduce.3
  485.4 38.4 %all-to-all-done.1 = f32[16,3,128,128]{3,2,1,0:T(8,128)S(1)} async-done(((f32[16,3,128,128]{3,2,1,0:T(8,128)}), f32[16,3,128,128]{3,2,1,0:T(8,128)S(1)}, u32[]{:S(2)}, u32[]{:S(2)}) %all-to-all-start.1) | async-done | bytes 3145760 | tf_op jit(solution)/shard_map/all_to_all | solution.py:110
  523.8 2.5 broadcast_in_dim.127
  526.3 10.1 scatter_fusion.3
  536.4 10.8 convolution_bitcast_fusion.4
  547.3 4.7 slice.10
  551.9 139.6 %all-reduce.2.cloned.1.call-done = f32[128,128]{1,0:T(8,128)} async-done(((f32[128,128]{1,0:T(8,128)}), f32[128,128]{1,0:T(8,128)}) %all-reduce.2.cloned.1.call-update) | async-done | bytes 65552 | tf_op jit(solution)/shard_map/psum | solution.py:125
  692.4 255.7 %while.52 = (s32[]{:T(128)}, f32[128,128]{1,0:T(8,128)S(1)}, f32[128,128]{1,0:T(8,128)S(1)}, s32[]{:T(128)}, s32[]{:T(128)}) while((s32[]{:T(128)}, f32[128,128]{1,0:T(8,128)S(1)}, f32[128,128]{1,0:T(8,128)S(1)}, s32[]{:T(128)}, s32[]{:T(128)}) %tuple.118), condition=%wide.region_15.16_spmd.clone.clone, body=%wide.region_13.15_spmd.clone.clone.sunk | while | flops 673410 | bytes 332909 | solution.py:26
  692.7 0.9 fusion.114
  694.7 0.9 fusion.114
  696.7 0.9 fusion.114
  698.7 0.9 fusion.114
  700.7 0.9 fusion.114
  702.7 0.9 fusion.114
  704.7 0.9 fusion.114
  706.7 0.9 fusion.114
  708.7 0.9 fusion.114
  710.6 0.9 fusion.114
  712.6 0.9 fusion.114
  714.6 0.9 fusion.114
  716.6 0.9 fusion.114
  720.6 0.9 fusion.114
  722.6 0.9 fusion.114
  724.6 0.9 fusion.114
  728.6 0.9 fusion.114
  730.6 0.9 fusion.114
  732.6 0.9 fusion.114
  948.8 231.7 %while.51 = (s32[]{:T(128)}, f32[128,128]{1,0:T(8,128)S(1)}, f32[128,128]{1,0:T(8,128)S(1)}, s32[]{:T(128)}, s32[]{:T(128)}) while((s32[]{:T(128)}, f32[128,128]{1,0:T(8,128)S(1)}, f32[128,128]{1,0:T(8,128)S(1)}, s32[]{:T(128)}, s32[]{:T(128)}) %tuple.121), condition=%wide.region_18.19_spmd.clone, body=%wide.region_16.18_spmd.clone.sunk | while | flops 460034 | bytes 265308 | solution.py:40
  1180.5 6.5 fusion.66
  (1315 shorter events, 378.1 us)
Async XLA Ops:
  7.2 203.1 %all-gather.2.cloned.1.call-start = ((), (), s32[]{:S(2)}) async-start(), calls=%async_computation.2 | async-start | bytes 35651584 | tf_op jit(solution)/shard_map/all_gather | solution.py:65
  10.0 468.3 %all-to-all-start = ((s32[16,1,3]{2,1,0:T(1,128)}), s32[16,1,3]{2,1,0:T(1,128)}, u32[]{:S(2)}, u32[]{:S(2)}) async-start(s32[16,1,3]{2,1,0:T(1,128)} %bitcast.12), calls=%async_computation | async-start | bytes 16384 | tf_op jit(solution)/shard_map/all_to_all | solution.py:61
  40.1 204.4 %copy-start = (s32[512]{0:T(512)S(1)}, s32[512]{0:T(512)}, u32[]{:S(2)}) copy-start(s32[512]{0:T(512)} %param.16) | copy-start | bytes 6148
  40.1 204.4 %copy-start.1 = (s32[512]{0:T(512)S(1)}, s32[512]{0:T(512)}, u32[]{:S(2)}) copy-start(s32[512]{0:T(512)} %param.15) | copy-start | bytes 6148
  478.3 45.5 %all-to-all-start.1 = ((f32[16,3,128,128]{3,2,1,0:T(8,128)}), f32[16,3,128,128]{3,2,1,0:T(8,128)S(1)}, u32[]{:S(2)}, u32[]{:S(2)}) async-start(f32[16,3,128,128]{3,2,1,0:T(8,128)} %bitcast.134), calls=%async_computation.1 | async-start | bytes 6291456 | tf_op jit(solution)/shard_map/all_to_all | solution.py:110
  483.2 208.3 %all-reduce.2.cloned.1.call-start = ((), (), s32[]{:S(2)}) async-start(), calls=%async_computation.3 | async-start | bytes 131072 | tf_op jit(solution)/shard_map/psum | solution.py:125
Sparse Core Ops, SparseCore 0:
  10.1 200.1 all-gather.1
  547.4 144.0 all-reduce.1
where the time goes:
time: 1200 us; the launch traced here: 1190 us
  matrix products  446 us (37%)
  waiting for transfers between devices  349 us (29%)
  other arithmetic  177 us (15%)
  loops' own time  98.1 us (8%)
  local copies, waits for them, and re-layouts  96.1 us (8%)
  between operations  14.2 us (1%)
  starting transfers between devices  13.7 us (1%)
    all_gather x1, waiting for transfers between devices, local(): shard_rows = lax.all_gather(sketch, 'dev', axis=0, tiled=True)  170 us
    psum x1, waiting for transfers between devices, local(): lax.psum(jnp.dot(normal.T, normal, precision=lax.Precision.HIGHEST), ('gr...  140 us
    dot_general x128, matrix products, column_step(): rest = target - jnp.dot(lower, row_part, precision=lax.Precision.HIGHEST)  113 us
    dot_general x128, matrix products, row_step(): jnp.dot(row_part, inverse, precision=lax.Precision.HIGHEST)  108 us
    dot_general x128, matrix products, row_step(): row_part = jnp.dot(pick, lower, precision=lax.Precision.HIGHEST)  107 us
    another operation x1, loops' own time, factor_lower(): lax.fori_loop(0, width, column_step, jnp.zeros((width, width), jnp.float32))  94 us
    scatter-add x4, other arithmetic, image_step(): return (running.at[ray_block].add(product), None)  68.2 us
    scatter-add x4, other arithmetic, normal_step(): return (running.at[col_block].add(product), None)  68.2 us
  transfers between devices with their start and end apart: 4, of which 3 were waited for; matrix products, arithmetic and copies ran while one was open for 25% of the time, Pallas kernels for 0%

commit v1 on v0

--- a/solution.py
+++ b/solution.py
@@ -122,8 +122,9 @@
         .add(arrived.reshape(slot_count, tile_size, width))
     )
     normal = normal[:block_count].reshape(block_count * tile_size, width)
-    gram_matrix = lax.psum(
-        jnp.dot(normal.T, normal, precision=lax.Precision.HIGHEST), ("grp", "dev")
+    gram_matrix = jnp.sum(
+        lax.all_gather(jnp.dot(normal.T, normal, precision=lax.Precision.HIGHEST), ("grp", "dev")),
+        axis=0,
     )
     voxels = normal.shape[0] * lax.axis_size("grp") * group_size
     gram_matrix = gram_matrix / voxels + gram_shift * jnp.eye(width, dtype=jnp.float32)

time: 1200 us -> 1130 us (0.942)
  waiting for transfers between devices: 349 us -> 279 us
    psum x1 -> x0, waiting for transfers between devices: 140 us -> none  [local(): lax.psum(jnp.dot(normal.T, normal, precision=lax.Precision.HIGHEST), ('gr...]
    all_gather x0 -> x1, waiting for transfers between devices: none -> 69.9 us  [local(): lax.all_gather(jnp.dot(normal.T, normal, precision=lax.Precision.HIGHEST)...]
  transfers between devices with their start and end apart: 4 -> 4, of which waited for: 3 -> 3; matrix products, arithmetic and copies ran while one was open for 25% -> 26% of each run, Pallas kernels for 0% -> 0%
where the time goes in v1:
time: 1130 us
  matrix products  446 us (39%)
  waiting for transfers between devices  279 us (25%)
  other arithmetic  180 us (16%)
  loops' own time  98.1 us (9%)
  local copies, waits for them, and re-layouts  96.1 us (9%)
  between operations  14.2 us (1%)
  starting transfers between devices  13.7 us (1%)
    all_gather x1, waiting for transfers between devices, local(): shard_rows = lax.all_gather(sketch, 'dev', axis=0, tiled=True)  170 us
    dot_general x128, matrix products, column_step(): rest = target - jnp.dot(lower, row_part, precision=lax.Precision.HIGHEST)  113 us
    dot_general x128, matrix products, row_step(): jnp.dot(row_part, inverse, precision=lax.Precision.HIGHEST)  108 us
    dot_general x128, matrix products, row_step(): row_part = jnp.dot(pick, lower, precision=lax.Precision.HIGHEST)  107 us
    another operation x1, loops' own time, factor_lower(): lax.fori_loop(0, width, column_step, jnp.zeros((width, width), jnp.float32))  94 us
    all_gather x1, waiting for transfers between devices, local(): lax.all_gather(jnp.dot(normal.T, normal, precision=lax.Precision.HIGHEST)...  69.9 us
    scatter-add x4, other arithmetic, image_step(): return (running.at[ray_block].add(product), None)  68.2 us
    scatter-add x4, other arithmetic, normal_step(): return (running.at[col_block].add(product), None)  68.2 us
  transfers between devices with their start and end apart: 4, of which 3 were waited for; matrix products, arithmetic and copies ran while one was open for 26% of the time, Pallas kernels for 0%

profile of v1, /device:TPU:1, one launch (start us, length us, event | category | flops | bytes accessed | tf_op | source)
XLA Modules:
  0.0 1126.4 jit_solution(3198701545785937318)
XLA Ops:
  7.9 1.0 select_reduce_fusion
  10.0 8.5 all-to-all-start
  18.5 21.4 %copy.22 = bf16[512,128,128]{1,2,0:T(8,128)(2,1)} copy(bf16[512,128,128]{2,1,0:T(8,128)(2,1)} %param.14) | data formatting | bytes 33554432 | tf_op args[0]
  40.1 170.2 %all-gather.4.cloned.1.call-done = bf16[131072,128]{1,0:T(8,128)(2,1)} async-done(((bf16[8192,128]{1,0:T(8,128)(2,1)}), bf16[131072,128]{1,0:T(8,128)(2,1)}) %all-gather.4.cloned.1.call-update) | async-done | bytes 33554448 | tf_op jit(solution)/shard_map/all_gather | solution.py:65
  210.3 32.8 %gather_fusion.2 = bf16[3072,128]{1,0:T(8,128)(2,1)S(1)} fusion(bf16[131072,128]{1,0:T(8,128)(2,1)} %all-gather.4.cloned.1.call-done, s32[3072]{0:T(1024)S(1)} %broadcast_clamp_fusion), kind=kCustom, calls=%fused_computation.2 | custom fusion | bytes 1585152 | tf_op jit(solution)/shard_map/jit(_take)/gather | solution.py:68
  243.1 1.2 select_select_fusion
  244.6 113.0 %while.49 = (s32[]{:T(128)}, f32[32,128,128]{2,1,0:T(8,128)S(1)}, s32[4,128]{1,0:T(4,128)S(1)}, bf16[4,128,128,128]{3,2,1,0:T(8,128)(2,1)}, s32[4,128]{1,0:T(4,1...) while((s32[]{:T(128)}, f32[32,128,128]{2,1,0:T(8,128)S(1)}, s32[4,128]{1,0:T(4,128)S(1)}, ...), condition=%wide.region_6.7_spmd, body=%wide.region_4.6_spmd.sunk | while | flops 541067776 | bytes 50340692 | solution.py:86
  244.6 3.1 gather_fusion
  247.7 8.0 fusion.97
  255.7 17.1 %scatter_fusion = f32[32,128,128]{2,1,0:T(8,128)S(1)} fusion(f32[32,128,128]{2,1,0:T(8,128)S(1)} %get-tuple-element.482, s32[128]{0:T(128)S(1)} %get-tuple-element.454, f32[128,128,128]{2,1,0:T(8,128)} %fusion.97), kind=kCustom, calls=%fused_computation.3.clone.1 | custom fusion | flops 2097152 | bytes 25166336 | tf_op jit(solution)/shard_map/while/body/eval_jaxpr/scatter-add | solution.py:84
  272.8 3.1 gather_fusion
  276.0 8.0 fusion.97
  284.0 17.1 %scatter_fusion = f32[32,128,128]{2,1,0:T(8,128)S(1)} fusion(f32[32,128,128]{2,1,0:T(8,128)S(1)} %get-tuple-element.482, s32[128]{0:T(128)S(1)} %get-tuple-element.454, f32[128,128,128]{2,1,0:T(8,128)} %fusion.97), kind=kCustom, calls=%fused_computation.3.clone.1 | custom fusion | flops 2097152 | bytes 25166336 | tf_op jit(solution)/shard_map/while/body/eval_jaxpr/scatter-add | solution.py:84
  301.1 3.1 gather_fusion
  304.2 8.0 fusion.97
  312.2 17.1 %scatter_fusion = f32[32,128,128]{2,1,0:T(8,128)S(1)} fusion(f32[32,128,128]{2,1,0:T(8,128)S(1)} %get-tuple-element.482, s32[128]{0:T(128)S(1)} %get-tuple-element.454, f32[128,128,128]{2,1,0:T(8,128)} %fusion.97), kind=kCustom, calls=%fused_computation.3.clone.1 | custom fusion | flops 2097152 | bytes 25166336 | tf_op jit(solution)/shard_map/while/body/eval_jaxpr/scatter-add | solution.py:84
  329.3 3.1 gather_fusion
  332.4 8.0 fusion.97
  340.5 17.0 %scatter_fusion = f32[32,128,128]{2,1,0:T(8,128)S(1)} fusion(f32[32,128,128]{2,1,0:T(8,128)S(1)} %get-tuple-element.482, s32[128]{0:T(128)S(1)} %get-tuple-element.454, f32[128,128,128]{2,1,0:T(8,128)} %fusion.97), kind=kCustom, calls=%fused_computation.3.clone.1 | custom fusion | flops 2097152 | bytes 25166336 | tf_op jit(solution)/shard_map/while/body/eval_jaxpr/scatter-add | solution.py:84
  357.9 112.9 %while.50 = (s32[]{:T(128)}, f32[24,128,128]{2,1,0:T(8,128)S(1)}, s32[4,128]{1,0:T(4,128)S(1)}, bf16[4,128,128,128]{2,3,1,0:T(8,128)(2,1)}, s32[4,128]{1,0:T(4,1...) while((s32[]{:T(128)}, f32[24,128,128]{2,1,0:T(8,128)S(1)}, s32[4,128]{1,0:T(4,128)S(1)}, ...), condition=%wide.region_9.10_spmd, body=%wide.region_7.9_spmd.sunk | while | flops 541067776 | bytes 50340692 | solution.py:101
  357.9 3.1 gather_fusion.1
  361.0 8.0 fusion.101
  369.0 17.0 %scatter_fusion.1 = f32[24,128,128]{2,1,0:T(8,128)S(1)} fusion(f32[24,128,128]{2,1,0:T(8,128)S(1)} %get-tuple-element.503, s32[128]{0:T(128)S(1)} %get-tuple-element.462, f32[128,128,128]{2,1,0:T(8,128)} %fusion.101), kind=kCustom, calls=%fused_computation.4.clone.1 | custom fusion | flops 2097152 | bytes 25166336 | tf_op jit(solution)/shard_map/while/body/eval_jaxpr/scatter-add | solution.py:99
  386.1 3.1 gather_fusion.1
  389.2 8.0 fusion.101
  397.3 17.1 %scatter_fusion.1 = f32[24,128,128]{2,1,0:T(8,128)S(1)} fusion(f32[24,128,128]{2,1,0:T(8,128)S(1)} %get-tuple-element.503, s32[128]{0:T(128)S(1)} %get-tuple-element.462, f32[128,128,128]{2,1,0:T(8,128)} %fusion.101), kind=kCustom, calls=%fused_computation.4.clone.1 | custom fusion | flops 2097152 | bytes 25166336 | tf_op jit(solution)/shard_map/while/body/eval_jaxpr/scatter-add | solution.py:99
  414.4 3.1 gather_fusion.1
  417.5 8.0 fusion.101
  425.5 17.0 %scatter_fusion.1 = f32[24,128,128]{2,1,0:T(8,128)S(1)} fusion(f32[24,128,128]{2,1,0:T(8,128)S(1)} %get-tuple-element.503, s32[128]{0:T(128)S(1)} %get-tuple-element.462, f32[128,128,128]{2,1,0:T(8,128)} %fusion.101), kind=kCustom, calls=%fused_computation.4.clone.1 | custom fusion | flops 2097152 | bytes 25166336 | tf_op jit(solution)/shard_map/while/body/eval_jaxpr/scatter-add | solution.py:99
  442.6 3.1 gather_fusion.1
  445.7 8.0 fusion.101
  453.7 17.0 %scatter_fusion.1 = f32[24,128,128]{2,1,0:T(8,128)S(1)} fusion(f32[24,128,128]{2,1,0:T(8,128)S(1)} %get-tuple-element.503, s32[128]{0:T(128)S(1)} %get-tuple-element.462, f32[128,128,128]{2,1,0:T(8,128)} %fusion.101), kind=kCustom, calls=%fused_computation.4.clone.1 | custom fusion | flops 2097152 | bytes 25166336 | tf_op jit(solution)/shard_map/while/body/eval_jaxpr/scatter-add | solution.py:99
  470.8 2.0 broadcast_in_dim.133
  472.8 5.4 scatter_fusion.2
  478.3 4.9 all-to-all-start.1
  484.0 1.4 reduce.3
  485.4 38.4 %all-to-all-done.1 = f32[16,3,128,128]{3,2,1,0:T(8,128)S(1)} async-done(((f32[16,3,128,128]{3,2,1,0:T(8,128)}), f32[16,3,128,128]{3,2,1,0:T(8,128)S(1)}, u32[]{:S(2)}, u32[]{:S(2)}) %all-to-all-start.1) | async-done | bytes 3145760 | tf_op jit(solution)/shard_map/all_to_all | solution.py:110
  523.8 2.5 broadcast_in_dim.127
  526.3 9.4 scatter_fusion.3
  535.7 10.8 convolution_bitcast_fusion.4
  546.6 4.6 slice.10
  551.2 69.9 %all-gather.6.cloned.1.call-done = f32[16384,128]{1,0:T(8,128)} async-done(((f32[128,128]{1,0:T(8,128)}), f32[16384,128]{1,0:T(8,128)}) %all-gather.6.cloned.1.call-update) | async-done | bytes 8388624 | tf_op jit(solution)/shard_map/all_gather | solution.py:126
  621.1 3.8 reduce_sum.78
  624.9 255.7 %while.52 = (s32[]{:T(128)}, f32[128,128]{1,0:T(8,128)S(1)}, f32[128,128]{1,0:T(8,128)S(1)}, s32[]{:T(128)}, s32[]{:T(128)}) while((s32[]{:T(128)}, f32[128,128]{1,0:T(8,128)S(1)}, f32[128,128]{1,0:T(8,128)S(1)}, s32[]{:T(128)}, s32[]{:T(128)}) %tuple.118), condition=%wide.region_15.16_spmd.clone.clone, body=%wide.region_13.15_spmd.clone.clone.sunk | while | flops 673410 | bytes 332909 | solution.py:26
  625.2 0.9 fusion.114
  627.2 0.9 fusion.114
  629.2 0.9 fusion.114
  631.2 0.9 fusion.114
  633.2 0.9 fusion.114
  635.2 0.9 fusion.114
  637.2 0.9 fusion.114
  639.2 0.9 fusion.114
  643.2 0.9 fusion.114
  645.2 0.9 fusion.114
  647.2 0.9 fusion.114
  651.2 0.9 fusion.114
  653.2 0.9 fusion.114
  655.2 0.9 fusion.114
  657.2 0.9 fusion.114
  659.2 0.9 fusion.114
  661.2 0.9 fusion.114
  663.2 0.9 fusion.114
  881.4 231.7 %while.51 = (s32[]{:T(128)}, f32[128,128]{1,0:T(8,128)S(1)}, f32[128,128]{1,0:T(8,128)S(1)}, s32[]{:T(128)}, s32[]{:T(128)}) while((s32[]{:T(128)}, f32[128,128]{1,0:T(8,128)S(1)}, f32[128,128]{1,0:T(8,128)S(1)}, s32[]{:T(128)}, s32[]{:T(128)}) %tuple.121), condition=%wide.region_18.19_spmd.clone, body=%wide.region_16.18_spmd.clone.sunk | while | flops 460034 | bytes 265308 | solution.py:40
  1113.0 6.5 fusion.66
  (1316 shorter events, 378.1 us)
Async XLA Ops:
  7.2 203.1 %all-gather.4.cloned.1.call-start = ((), (), s32[]{:S(2)}) async-start(), calls=%async_computation.2 | async-start | bytes 35651584 | tf_op jit(solution)/shard_map/all_gather | solution.py:65
  10.0 468.3 %all-to-all-start = ((s32[16,1,3]{2,1,0:T(1,128)}), s32[16,1,3]{2,1,0:T(1,128)}, u32[]{:S(2)}, u32[]{:S(2)}) async-start(s32[16,1,3]{2,1,0:T(1,128)} %bitcast.12), calls=%async_computation | async-start | bytes 16384 | tf_op jit(solution)/shard_map/all_to_all | solution.py:61
  40.1 204.4 %copy-start = (s32[512]{0:T(512)S(1)}, s32[512]{0:T(512)}, u32[]{:S(2)}) copy-start(s32[512]{0:T(512)} %param.16) | copy-start | bytes 6148
  40.1 204.4 %copy-start.1 = (s32[512]{0:T(512)S(1)}, s32[512]{0:T(512)}, u32[]{:S(2)}) copy-start(s32[512]{0:T(512)} %param.15) | copy-start | bytes 6148
  478.3 45.5 %all-to-all-start.1 = ((f32[16,3,128,128]{3,2,1,0:T(8,128)}), f32[16,3,128,128]{3,2,1,0:T(8,128)S(1)}, u32[]{:S(2)}, u32[]{:S(2)}) async-start(f32[16,3,128,128]{3,2,1,0:T(8,128)} %bitcast.135), calls=%async_computation.1 | async-start | bytes 6291456 | tf_op jit(solution)/shard_map/all_to_all | solution.py:110
  483.2 137.9 %all-gather.6.cloned.1.call-start = ((), (), s32[]{:S(2)}) async-start(), calls=%async_computation.3 | async-start | bytes 8454144 | tf_op jit(solution)/shard_map/all_gather | solution.py:126
Sparse Core Ops, SparseCore 0:
  10.1 200.1 all-gather.3
  546.7 74.3 all-gather.5
